TPU v7x, 128 devices: a whole 4x4x4 slice. The times are simulated.
128 devices in a mesh: band: 4 (over z_lo, core), pos: 32 (over z_hi, y, x).
Axes of the slice: x: 4, y: 4, z: 4 (z_hi: 2, z_lo: 2; z = z_hi * 2 + z_lo), core: 2. Of those that a mesh axis runs over, the one named last changes fastest.
Arguments:
- input_map: bfloat16 [1, 32, 4, 64, 4096], P(None, 'pos', 'band'), may hold values from -6 to 6
- cotangent: bfloat16 [1, 32, 4, 64, 4096], P(None, 'pos', 'band'), may hold values from -6 to 6
- band_width: int32 [32], P('pos'), may hold values from 2 to 3
- dilation: int32 [2], replicated, may hold values from 1 to 16, as said below
- conv_weight: bfloat16 [2, 64, 576], replicated, may hold values from -0.25 to 0.25
- conv_bias: float32 [2, 64], replicated, may hold values from -3 to 3
Outputs:
- output_map: bfloat16 [1, 32, 4, 64, 4096], P(None, 'pos', 'band')
- input_grad: float32 [1, 32, 4, 64, 4096], P(None, 'pos', 'band')
- weight_grad: float32 [2, 64, 576], replicated
- bias_grad: float32 [2, 64], replicated
Inputs may be any that keep to these rules, and one draw needn't show every extreme that they name: Some layer has dilation exactly 16.
All inputs are finite; a program needn't handle non-finite values.
Results may differ from a plain program's by a relative error of at most 0.0075.
Values may be sent and summed in bfloat16 or wider, within the bound.
A program may use at most 128 MiB of HBM per device.

v0:
```python
import math

import jax
import jax.numpy as jnp
import numpy as np
from jax import lax
from jax.sharding import PartitionSpec as P

BLOCK = 64
DMAX = 16
LAYERS = 2


tap_order = np.array([0, 3, 6, 1, 4, 7, 2, 5, 8])


def from_behind(value, axis, steps):
    count = lax.axis_size(axis)
    first, last = (max(0, -steps), min(count, count - steps))
    return lax.ppermute(value, axis, [(source, source + steps) for source in range(first, last)])


def shift_band(payload, shift_by):
    return from_behind(payload, "band", shift_by)


def shift_rows(strip_rows, corners, shift_by):
    return from_behind((strip_rows, corners), "pos", shift_by)


def own_parts(stored):
    leading = stored.shape[:-2]
    flat_shape = leading + (DMAX * DMAX,)
    top_rows = stored[..., :DMAX, :]
    bottom_rows = stored[..., -DMAX:, :]
    left_cols = jnp.swapaxes(stored[..., :DMAX], -1, -2)
    right_cols = jnp.swapaxes(stored[..., -DMAX:], -1, -2)
    low_corner = stored[..., -DMAX:, :DMAX].reshape(flat_shape)
    high_corner = stored[..., :DMAX, -DMAX:].reshape(flat_shape)
    lower_right = stored[..., -DMAX:, -DMAX:].reshape(flat_shape)
    upper_left = stored[..., :DMAX, :DMAX].reshape(flat_shape)
    return (
        top_rows,
        bottom_rows,
        left_cols,
        right_cols,
        low_corner,
        high_corner,
        lower_right,
        upper_left,
    )


def assemble(stored, pieces, block_offset):
    (
        from_above,
        from_right,
        from_left,
        from_below,
        corner_above,
        far_above,
        far_below,
        corner_below,
    ) = pieces
    square = corner_above.shape[:-1] + (DMAX, DMAX)
    far_up = far_above.reshape(square)
    own_low = jnp.swapaxes(stored[..., -DMAX:, :DMAX], -1, -2)
    down_left = jnp.where(
        block_offset == 0,
        jnp.swapaxes(far_up, -1, -2),
        jnp.where(block_offset == 1, own_low, far_below.reshape(square)),
    )
    lower_rim = jnp.where(block_offset == 0, from_right, from_below)
    left_rim = jnp.where(block_offset == 0, from_above, from_left)
    upper = jnp.concatenate([corner_above.reshape(square), from_above, far_up], axis=-1)
    middle = jnp.concatenate(
        [jnp.swapaxes(left_rim, -1, -2), stored, jnp.swapaxes(from_right, -1, -2)], axis=-1
    )
    lower = jnp.concatenate([down_left, lower_rim, corner_below.reshape(square)], axis=-1)
    return jnp.concatenate([upper, middle, lower], axis=-2)


def patches(framed, spread):
    channels = framed.shape[0]
    edge_bins = framed.shape[1] - 2 * DMAX
    anchor = spread * 0
    windows = []
    for row_tap in range(3):
        for col_tap in range(3):
            start_row = DMAX + (row_tap - 1) * spread
            start_col = DMAX + (col_tap - 1) * spread
            windows.append(
                lax.dynamic_slice(
                    framed, (anchor, start_row, start_col), (channels, edge_bins, edge_bins)
                )
            )
    return jnp.stack(windows, 0).reshape(9 * channels, edge_bins * edge_bins)


def paired(weight):
    channels = weight.shape[0]
    turned = weight.reshape(channels, 9, channels)[:, tap_order, :].reshape(channels, 9 * channels)
    return jnp.concatenate([weight, turned], axis=0)


def fold_pair(pair_grad):
    channels = pair_grad.shape[0] // 2
    turned = (
        pair_grad[channels:]
        .reshape(channels, 9, channels)[:, tap_order, :]
        .reshape(channels, 9 * channels)
    )
    return pair_grad[:channels] + turned


def forward_block(framed, stored, weight_pair, bias_pair, kept_block, spread):
    channels, edge_bins = (stored.shape[0], stored.shape[1])
    columns = patches(framed, spread)
    mixed_sum = (
        jnp.dot(weight_pair, columns, preferred_element_type=jnp.float32) + bias_pair[:, None]
    )
    active = 0.5 * (jax.nn.gelu(mixed_sum[:channels]) + jax.nn.gelu(mixed_sum[channels:]))
    return (
        kept_block * (stored.astype(jnp.float32) + active.reshape(channels, edge_bins, edge_bins))
    ).astype(jnp.bfloat16)


def backward_block(framed, gradient, weight_pair, bias_pair, kept_block, spread):
    channels, edge_bins = (gradient.shape[0], gradient.shape[1])
    columns = patches(framed, spread)
    mixed_sum = (
        jnp.dot(weight_pair, columns, preferred_element_type=jnp.float32) + bias_pair[:, None]
    )
    masked = kept_block * gradient
    half_grad = 0.5 * masked.reshape(channels, edge_bins * edge_bins)
    slope_grad = jax.vjp(jax.nn.gelu, mixed_sum)[1](
        jnp.concatenate([half_grad, half_grad], axis=0)
    )[0]
    slope_low = slope_grad.astype(jnp.bfloat16)
    pair_grad = lax.dot_general(
        slope_low, columns, (((1,), (1,)), ((), ())), preferred_element_type=jnp.float32
    )
    bias_term = jnp.sum(slope_grad, axis=1)
    column_grad = lax.dot_general(
        weight_pair, slope_low, (((0,), (0,)), ((), ())), preferred_element_type=jnp.float32
    )
    pullback = jax.vjp(lambda whole: patches(whole, spread), framed.astype(jnp.float32))[1]
    tile_grad = pullback(column_grad)[0]
    return (masked, tile_grad, pair_grad, bias_term)


def per_device(input_map, cotangent, band_width, dilation, conv_weight, conv_bias):
    samples, channels = (input_map.shape[0], input_map.shape[3])
    edge_bins = BLOCK
    block_shape = (samples, channels, edge_bins, edge_bins)
    rows_all = lax.axis_size("pos")
    offsets_all = lax.axis_size("band")
    block_row = lax.axis_index("pos")
    block_offset = lax.axis_index("band")
    inside = (block_offset <= band_width[0]) & (block_row + block_offset < rows_all)
    kept_block = jnp.where(inside, 1.0, 0.0).astype(jnp.float32)
    zero_block = jnp.zeros(block_shape, jnp.float32)
    strip_zero = jnp.zeros((samples, channels, DMAX, edge_bins), jnp.float32)
    corner_zero = jnp.zeros((samples, channels, DMAX * DMAX), jnp.float32)
    zero_pieces = (strip_zero,) * 4 + (corner_zero,) * 4

    def retract(grads):
        (
            from_above,
            from_right,
            from_left,
            from_below,
            corner_above,
            far_above,
            far_below,
            corner_below,
        ) = grads
        back_above, corners_up = shift_rows(from_above, jnp.stack([corner_above, far_above]), -1)
        back_below, corners_down = shift_rows(from_below, jnp.stack([corner_below, far_below]), 1)
        band_after = shift_band(jnp.stack([back_above, from_right]), 1)
        band_before = shift_band(jnp.stack([back_below, from_left]), -1)
        low_back = shift_band(corners_up[1], 2)
        high_back = shift_band(corners_down[1], -2)
        sent = (
            band_before[0],
            band_after[0],
            band_after[1],
            band_before[1],
            low_back,
            high_back,
            corners_up[0],
            corners_down[0],
        )
        pullback = jax.vjp(own_parts, zero_block)[1]
        return pullback(tuple((piece.astype(jnp.float32) for piece in sent)))[0]

    current = (input_map.reshape(block_shape).astype(jnp.float32) * kept_block).astype(jnp.bfloat16)
    stored_layers = []
    framed_layers = []
    for layer_index in range(LAYERS):
        weight_pair = paired(conv_weight[layer_index])
        bias_pair = jnp.concatenate([conv_bias[layer_index], conv_bias[layer_index]])
        spread = dilation[layer_index]
        (
            top_rows,
            bottom_rows,
            left_cols,
            right_cols,
            low_corner,
            high_corner,
            lower_right,
            upper_left,
        ) = own_parts(current)
        extend_band_after = shift_band(jnp.stack([bottom_rows, left_cols]), -1)
        extend_band_before = shift_band(jnp.stack([top_rows, right_cols]), 1)
        far_after = shift_band(low_corner, -2)
        far_before = shift_band(high_corner, 2)
        extend_from_above, extend_corners_up = shift_rows(
            extend_band_after[0], jnp.stack([lower_right, far_after]), 1
        )
        extend_from_below, extend_corners_down = shift_rows(
            extend_band_before[0], jnp.stack([upper_left, far_before]), -1
        )
        extend_from_right = extend_band_after[1]
        extend_from_left = extend_band_before[1]
        extend_corner_above = extend_corners_up[0]
        extend_far_above = extend_corners_up[1]
        extend_corner_below = extend_corners_down[0]
        extend_far_below = extend_corners_down[1]
        extend_pieces = (
            extend_from_above,
            extend_from_right,
            extend_from_left,
            extend_from_below,
            extend_corner_above,
            extend_far_above,
            extend_far_below,
            extend_corner_below,
        )
        framed = assemble(current, extend_pieces, block_offset)
        stored_layers.append(current)
        framed_layers.append(framed)
        current = lax.map(
            lambda element: forward_block(
                element[0], element[1], weight_pair, bias_pair, kept_block, spread
            ),
            (framed, current),
        )
    gradient = cotangent.reshape(block_shape).astype(jnp.float32)
    weight_terms = [None] * LAYERS
    bias_terms = [None] * LAYERS
    assemble_back = jax.vjp(
        lambda whole, pieces: assemble(whole, pieces, block_offset), zero_block, zero_pieces
    )[1]
    for layer_index in reversed(range(LAYERS)):
        weight_pair = paired(conv_weight[layer_index])
        bias_pair = jnp.concatenate([conv_bias[layer_index], conv_bias[layer_index]])
        spread = dilation[layer_index]
        framed = framed_layers[layer_index]
        masked, tile_grad, pair_grad, bias_term = lax.map(
            lambda element: backward_block(
                element[0], element[1], weight_pair, bias_pair, kept_block, spread
            ),
            (framed, gradient),
        )
        weight_terms[layer_index] = fold_pair(jnp.sum(pair_grad, axis=0))
        bias_both = jnp.sum(bias_term, axis=0)
        bias_terms[layer_index] = bias_both[:channels] + bias_both[channels:]
        block_grad, piece_grads = assemble_back(tile_grad)
        rounded = tuple((piece.astype(jnp.bfloat16) for piece in piece_grads))
        gradient = masked + block_grad + retract(rounded)
    input_grad = gradient * kept_block
    weight_sum, bias_sum = lax.psum(
        (jnp.stack(weight_terms), jnp.stack(bias_terms)), ("band", "pos")
    )
    scale = 1.0 / (edge_bins * math.sqrt(samples * rows_all * offsets_all))
    return (
        current.reshape(input_map.shape),
        input_grad.reshape(input_map.shape),
        weight_sum * scale,
        bias_sum * scale,
    )


def solution(mesh):
    placed = (
        P(None, "pos", "band", None, None),
        P(None, "pos", "band", None, None),
        P("pos"),
        P(),
        P(),
        P(),
    )
    return jax.shard_map(
        per_device,
        mesh=mesh,
        in_specs=placed,
        out_specs=(
            P(None, "pos", "band", None, None),
            P(None, "pos", "band", None, None),
            P(),
            P(),
        ),
        check_vma=False,
    )
```

profile of v0, /device:TPU:1, one launch (start us, length us, event | category | flops | bytes accessed | tf_op | source)
XLA Modules:
  0.0 900.1 jit_solution(15067481776046239439)
XLA Ops:
  15.2 5.6 collective-permute-start.5
  98.7 13.6 %reshape.603 = bf16[576,4096]{1,0:T(8,128)(2,1)} reshape(bf16[9,64,64,64]{3,2,1,0:T(8,128)(2,1)} %dynamic-slice_dynamic-update-slice_fusion.8) | data formatting | bytes 9437184 | tf_op jit(solution)/shard_map/while/body/eval_jaxpr/reshape | solution.py:97
  125.3 4.6 collective-permute-start.10
  144.0 5.8 collective-permute-done.14
  156.3 6.5 collective-permute-done.15
  162.9 14.2 %maximum_maximum_fusion = bf16[1,64,96,96]{1,2,3,0:T(8,128)(2,1)S(1)} fusion(bf16[1,64,16,16]{1,2,3,0:T(8,128)(2,1)S(1)} %copy.212, bf16[1,64,16,64]{1,2,3,0:T(8,128)(2,1)S(1)} %bitcast_select_fusion, bf16[1,64,16,16]{1,2,3,0:T(8,128)(2,1)S(1)} %copy.211, bf16[1,64,64,16]{1,2,3,0:T(8,128)(2,1)S(1)} %copy.206, ...), kind=kLoop, calls=%fused_computation.12 | loop fusion | flops 10616832 | bytes 2359296 | tf_op jit(solution)/shard_map/concatenate | solution.py:80
  182.4 14.2 %fusion.128 = bf16[64,96,96]{0,1,2:T(8,128)(2,1)S(1)} fusion(bf16[1,64,16,16]{1,2,3,0:T(8,128)(2,1)S(1)} %copy.212, bf16[1,64,16,64]{1,2,3,0:T(8,128)(2,1)S(1)} %bitcast_select_fusion, bf16[1,64,16,16]{1,2,3,0:T(8,128)(2,1)S(1)} %copy.211, bf16[1,64,64,16]{1,2,3,0:T(8,128)(2,1)S(1)} %copy.206, bf16[1,64,64,64]{1,2,3,0:T(8,128)(2,1)S(1)} %multiply_convert_fusion, ...), kind=kLoop, calls=%fused_computation.266 | loop fusion | flops 10616832 | bytes 2359296 | tf_op jit(solution)/shard_map/while/body/jit(dynamic_index_in_dim)/squeeze | solution.py:243
  203.0 17.0 %copy.213 = bf16[9,64,64,64]{3,2,1,0:T(8,128)(2,1)} copy(bf16[9,64,64,64]{1,2,3,0:T(8,128)(2,1)} %dynamic-slice_dynamic-update-slice_fusion) | data formatting | bytes 9437184 | tf_op jit(solution)/shard_map/while/body/eval_jaxpr/stack | solution.py:97
  220.0 13.2 %reshape.608 = bf16[576,4096]{1,0:T(8,128)(2,1)} reshape(bf16[9,64,64,64]{3,2,1,0:T(8,128)(2,1)} %copy.213) | data formatting | bytes 9437184 | tf_op jit(solution)/shard_map/while/body/eval_jaxpr/reshape | solution.py:97
  233.2 6.0 fusion.99
  261.7 4.6 copy.216
  269.0 11.2 %dynamic_update_slice.101 = f32[64,96,96]{0,1,2:T(8,128)} dynamic-update-slice(f32[64,96,96]{0,1,2:T(8,128)} %broadcast.183.clone, f32[64,64,64]{0,1,2:T(8,128)} %copy.214, s32[]{:T(128)} %constant.189.clone.1, s32[]{:T(128)S(6)} %select_n.251, s32[]{:T(128)S(6)} %select_n.251) | dynamic-update-slice | bytes 2097156 | tf_op jit(solution)/shard_map/while/body/eval_jaxpr/transpose(jvp())/dynamic_update_slice | solution.py:93
  284.4 11.2 %add_any.172 = f32[64,96,96]{0,1,2:T(8,128)} dynamic-update-slice(f32[64,96,96]{0,1,2:T(8,128)} %dynamic_update_slice.101, f32[64,64,64]{0,1,2:T(8,128)} %dynamic-slice_add_fusion.7, s32[]{:T(128)} %constant.189.clone.1, s32[]{:T(128)S(6)} %select_n.251, s32[]{:T(128)} %constant.194.clone.1) | dynamic-update-slice | bytes 2097156 | tf_op jit(solution)/shard_map/while/body/eval_jaxpr/transpose(jvp())/add_any | solution.py:93
  299.7 11.2 %add_any.174 = f32[64,96,96]{0,1,2:T(8,128)} dynamic-update-slice(f32[64,96,96]{0,1,2:T(8,128)} %add_any.172, f32[64,64,64]{0,1,2:T(8,128)} %dynamic-slice_add_fusion.6, s32[]{:T(128)} %constant.189.clone.1, s32[]{:T(128)S(6)} %select_n.251, s32[]{:T(128)S(6)} %select_n.250) | dynamic-update-slice | bytes 2097156 | tf_op jit(solution)/shard_map/while/body/eval_jaxpr/transpose(jvp())/add_any | solution.py:93
  351.6 11.5 %add_any.181 = f32[64,96,96]{0,1,2:T(8,128)} dynamic-update-slice(f32[64,96,96]{0,1,2:T(8,128)} %copy-done.2, f32[64,64,64]{0,1,2:T(8,128)} %dynamic-slice_add_fusion.5, s32[]{:T(128)} %constant.189.clone.1, s32[]{:T(128)S(6)} %select_n.250, s32[]{:T(128)S(6)} %select_n.251) | dynamic-update-slice | bytes 2097156 | tf_op jit(solution)/shard_map/while/body/eval_jaxpr/transpose(jvp())/add_any | solution.py:93
  374.7 11.4 %add_any.183 = f32[64,96,96]{0,1,2:T(8,128)} dynamic-update-slice(f32[64,96,96]{0,1,2:T(8,128)} %add_any.181, f32[64,64,64]{0,1,2:T(8,128)} %dynamic-slice_add_fusion.4, s32[]{:T(128)} %constant.189.clone.1, s32[]{:T(128)S(6)} %select_n.250, s32[]{:T(128)} %constant.194.clone.1) | dynamic-update-slice | bytes 2097156 | tf_op jit(solution)/shard_map/while/body/eval_jaxpr/transpose(jvp())/add_any | solution.py:93
  396.6 11.4 %add_any.185 = f32[1,64,96,96]{1,2,3,0:T(8,128)} dynamic-update-slice(f32[1,64,96,96]{1,2,3,0:T(8,128)} %bitcast.259, f32[1,64,64,64]{1,2,3,0:T(8,128)} %add_bitcast_fusion.1, s32[]{:T(128)} %constant.189.clone.1, s32[]{:T(128)} %constant.189.clone.1, s32[]{:T(128)S(6)} %select_n.250, s32[]{:T(128)S(6)} %select_n.250) | dynamic-update-slice | bytes 2097156 | tf_op jit(solution)/shard_map/while/body/eval_jaxpr/transpose(jvp())/add_any | solution.py:93
  418.1 5.7 collective-permute-start.16
  438.9 4.6 collective-permute-start.20
  446.7 7.2 collective-permute-start.19
  464.0 4.6 collective-permute-done.21
  501.6 10.2 %dynamic_update_slice.111 = f32[64,96,96]{0,1,2:T(8,128)} dynamic-update-slice(f32[64,96,96]{0,1,2:T(8,128)} %broadcast.183, f32[64,64,64]{0,1,2:T(8,128)S(1)} %copy.241, s32[]{:T(128)} %constant.189.clone.1, s32[]{:T(128)S(6)} %select_n.244, s32[]{:T(128)S(6)} %select_n.244) | dynamic-update-slice | bytes 2097156 | tf_op jit(solution)/shard_map/while/body/eval_jaxpr/transpose(jvp())/dynamic_update_slice | solution.py:93
  514.5 10.2 %add_any.199 = f32[64,96,96]{0,1,2:T(8,128)} dynamic-update-slice(f32[64,96,96]{0,1,2:T(8,128)} %dynamic_update_slice.111, f32[64,64,64]{0,1,2:T(8,128)S(1)} %dynamic-slice_add_fusion.3, s32[]{:T(128)} %constant.189.clone.1, s32[]{:T(128)S(6)} %select_n.244, s32[]{:T(128)} %constant.194.clone.1) | dynamic-update-slice | bytes 2097156 | tf_op jit(solution)/shard_map/while/body/eval_jaxpr/transpose(jvp())/add_any | solution.py:93
  532.4 10.3 %add_any.201 = f32[64,96,96]{0,1,2:T(8,128)} dynamic-update-slice(f32[64,96,96]{0,1,2:T(8,128)} %add_any.199, f32[64,64,64]{0,1,2:T(8,128)S(1)} %dynamic-slice_add_fusion.2, s32[]{:T(128)} %constant.189.clone.1, s32[]{:T(128)S(6)} %select_n.244, s32[]{:T(128)S(6)} %select_n.243) | dynamic-update-slice | bytes 2097156 | tf_op jit(solution)/shard_map/while/body/eval_jaxpr/transpose(jvp())/add_any | solution.py:93
  580.6 10.8 %add_any.208 = f32[64,96,96]{0,1,2:T(8,128)} dynamic-update-slice(f32[64,96,96]{0,1,2:T(8,128)} %copy-done, f32[64,64,64]{0,1,2:T(8,128)S(1)} %dynamic-slice_add_fusion.1, s32[]{:T(128)} %constant.189.clone.1, s32[]{:T(128)S(6)} %select_n.243, s32[]{:T(128)S(6)} %select_n.244) | dynamic-update-slice | bytes 2097156 | tf_op jit(solution)/shard_map/while/body/eval_jaxpr/transpose(jvp())/add_any | solution.py:93
  599.3 10.9 %add_any.210 = f32[64,96,96]{0,1,2:T(8,128)} dynamic-update-slice(f32[64,96,96]{0,1,2:T(8,128)} %add_any.208, f32[64,64,64]{0,1,2:T(8,128)S(1)} %dynamic-slice_add_fusion, s32[]{:T(128)} %constant.189.clone.1, s32[]{:T(128)S(6)} %select_n.243, s32[]{:T(128)} %constant.194.clone.1) | dynamic-update-slice | bytes 2097156 | tf_op jit(solution)/shard_map/while/body/eval_jaxpr/transpose(jvp())/add_any | solution.py:93
  619.1 11.4 %add_any.212 = f32[1,64,96,96]{1,2,3,0:T(8,128)} dynamic-update-slice(f32[1,64,96,96]{1,2,3,0:T(8,128)} %bitcast.258, f32[1,64,64,64]{1,2,3,0:T(8,128)} %add_bitcast_fusion, s32[]{:T(128)} %constant.189.clone.1, s32[]{:T(128)} %constant.189.clone.1, s32[]{:T(128)S(6)} %select_n.243, s32[]{:T(128)S(6)} %select_n.243) | dynamic-update-slice | bytes 2097156 | tf_op jit(solution)/shard_map/while/body/eval_jaxpr/transpose(jvp())/add_any | solution.py:93
  637.5 91.7 %psum.15 = f32[2,64]{1,0:T(2,128)S(1)} all-reduce(f32[2,64]{1,0:T(2,128)S(1)} %pad_maximum_fusion.28), channel_id=1, replica_groups=mesh['band'=4,'pos'=32] {'band','pos'}, use_global_device_ids=true, to_apply=%region_3.4 | all-reduce | flops 128 | bytes 1024 | tf_op jit(solution)/shard_map/psum | solution.py:273
  750.7 5.2 collective-permute-start.27
  756.8 4.5 collective-permute-start.29
  764.1 113.3 %all-reduce.22.cloned.1.call-done = f32[2,64,576]{1,2,0:T(8,128)} async-done(((f32[2,64,576]{1,2,0:T(8,128)}), f32[2,64,576]{1,2,0:T(8,128)}) %all-reduce.22.cloned.1.call-update) | async-done | bytes 294928 | tf_op jit(solution)/shard_map/psum | solution.py:273
  884.0 5.8 fusion.23
  (367 shorter events, 400.2 us)
Async XLA Ops:
  7.2 870.2 %all-reduce.22.cloned.1.call-start = ((), (), s32[]{:S(2)}) async-start(), calls=%async_computation | async-start | bytes 1179648 | tf_op jit(solution)/shard_map/psum | solution.py:273
  13.0 39.1 %collective-permute-start = (bf16[1,64,256]{1,2,0:T(8,128)(2,1)S(1)}, bf16[1,64,256]{1,2,0:T(8,128)(2,1)}, u32[]{:S(2)}, u32[]{:S(2)}) collective-permute-start(bf16[1,64,256]{1,2,0:T(8,128)(2,1)S(1)} %bitcast.289), channel_id=1, source_target_pairs={{64,0},{96,32},{65,1},{97,33},{66,2},{98,34},{67,3},{99,35},{68,4}... | collective-permute-start | bytes 98312 | tf_op jit(solution)/shard_map/ppermute | solution.py:20
  15.2 41.4 %collective-permute-start.5 = (bf16[1,64,256]{1,2,0:T(8,128)(2,1)}, bf16[1,64,256]{1,2,0:T(8,128)(2,1)}, u32[]{:S(2)}, u32[]{:S(2)}) collective-permute-start(bf16[1,64,256]{1,2,0:T(8,128)(2,1)} %bitcast.25), channel_id=1, source_target_pairs={{0,64},{32,96},{1,65},{33,97},{2,66},{34,98},{3,67},{35,99},{4,68}... | collective-permute-start | bytes 98312 | tf_op jit(solution)/shard_map/ppermute | solution.py:20
  29.4 36.8 %collective-permute-start.2 = (bf16[2,1,64,16,64]{2,3,4,1,0:T(8,128)(2,1)}, bf16[2,1,64,16,64]{2,3,4,1,0:T(8,128)(2,1)}, u32[]{:S(2)}, u32[]{:S(2)}) collective-permute-start(bf16[2,1,64,16,64]{2,3,4,1,0:T(8,128)(2,1)} %pad_maximum_fusion.4), channel_id=1, source_target_pairs={{32,0},{64,32},{96,64},{33,1},{65,33},{97,65},{34,2},{66,34},{98,6... | collective-permute-start | bytes 786440 | tf_op jit(solution)/shard_map/ppermute | solution.py:20
  35.0 29.0 %collective-permute-start.4 = (bf16[2,1,64,16,64]{2,3,4,1,0:T(8,128)(2,1)}, bf16[2,1,64,16,64]{2,3,4,1,0:T(8,128)(2,1)}, u32[]{:S(2)}, u32[]{:S(2)}) collective-permute-start(bf16[2,1,64,16,64]{2,3,4,1,0:T(8,128)(2,1)} %pad_maximum_fusion.5), channel_id=1, source_target_pairs={{0,32},{32,64},{64,96},{1,33},{33,65},{65,97},{2,34},{34,66},{66,9... | collective-permute-start | bytes 786440 | tf_op jit(solution)/shard_map/ppermute | solution.py:20
  53.0 5.8 collective-permute-start.1
  64.9 9.1 %collective-permute-start.7 = (bf16[1,64,16,64]{1,2,3,0:T(8,128)(2,1)S(1)}, bf16[1,64,16,64]{1,2,3,0:T(8,128)(2,1)}, u32[]{:S(2)}, u32[]{:S(2)}) collective-permute-start(bf16[1,64,16,64]{1,2,3,0:T(8,128)(2,1)S(1)} %slice_bitcast_fusion.17), channel_id=1, source_target_pairs={{1,0},{2,1},{3,2},{4,3},{5,4},{6,5},{7,6},{8,7},{9,8},{10,9},{11,1... | collective-permute-start | bytes 393224 | tf_op jit(solution)/shard_map/ppermute | solution.py:20
  68.0 9.2 %collective-permute-start.3 = (bf16[1,64,16,64]{1,2,3,0:T(8,128)(2,1)}, bf16[1,64,16,64]{1,2,3,0:T(8,128)(2,1)S(1)}, u32[]{:S(2)}, u32[]{:S(2)}) collective-permute-start(bf16[1,64,16,64]{1,2,3,0:T(8,128)(2,1)} %get-tuple-element.194), channel_id=1, source_target_pairs={{0,1},{1,2},{2,3},{3,4},{4,5},{5,6},{6,7},{7,8},{8,9},{9,10},{10,1... | collective-permute-start | bytes 393224 | tf_op jit(solution)/shard_map/ppermute | solution.py:20
  125.3 24.5 %collective-permute-start.10 = (bf16[2,1,64,16,64]{2,3,4,1,0:T(8,128)(2,1)S(1)}, bf16[2,1,64,16,64]{2,3,4,1,0:T(8,128)(2,1)S(1)}, u32[]{:S(2)}, u32[]{:S(2)}) collective-permute-start(bf16[2,1,64,16,64]{2,3,4,1,0:T(8,128)(2,1)S(1)} %pad_maximum_fusion.6), channel_id=1, source_target_pairs={{32,0},{64,32},{96,64},{33,1},{65,33},{97,65},{34,2},{66,34},{98,6... | collective-permute-start | bytes 786440 | tf_op jit(solution)/shard_map/ppermute | solution.py:20
  130.1 6.8 collective-permute-start.8
  131.6 21.4 %collective-permute-start.12 = (bf16[2,1,64,16,64]{2,3,4,1,0:T(8,128)(2,1)S(1)}, bf16[2,1,64,16,64]{2,3,4,1,0:T(8,128)(2,1)S(1)}, u32[]{:S(2)}, u32[]{:S(2)}) collective-permute-start(bf16[2,1,64,16,64]{2,3,4,1,0:T(8,128)(2,1)S(1)} %pad_maximum_fusion.7), channel_id=1, source_target_pairs={{0,32},{32,64},{64,96},{1,33},{33,65},{65,97},{2,34},{34,66},{66,9... | collective-permute-start | bytes 786440 | tf_op jit(solution)/shard_map/ppermute | solution.py:20
  135.2 7.5 collective-permute-start.13
  137.0 7.0 collective-permute-start.9
  142.6 7.1 collective-permute-start.14
  149.9 6.2 collective-permute-start.11
  153.0 9.8 %collective-permute-start.15 = (bf16[1,64,16,64]{1,2,3,0:T(8,128)(2,1)S(1)}, bf16[1,64,16,64]{1,2,3,0:T(8,128)(2,1)S(1)}, u32[]{:S(2)}, u32[]{:S(2)}) collective-permute-start(bf16[1,64,16,64]{1,2,3,0:T(8,128)(2,1)S(1)} %slice_bitcast_fusion.12), channel_id=1, source_target_pairs={{1,0},{2,1},{3,2},{4,3},{5,4},{6,5},{7,6},{8,7},{9,8},{10,9},{11,1... | collective-permute-start | bytes 393224 | tf_op jit(solution)/shard_map/ppermute | solution.py:20
  418.1 25.5 %collective-permute-start.16 = (bf16[2,1,64,256]{2,3,1,0:T(8,128)(2,1)}, bf16[2,1,64,256]{2,3,1,0:T(8,128)(2,1)}, u32[]{:S(2)}, u32[]{:S(2)}) collective-permute-start(bf16[2,1,64,256]{2,3,1,0:T(8,128)(2,1)} %pad_maximum_fusion.20), channel_id=1, source_target_pairs={{0,1},{1,2},{2,3},{3,4},{4,5},{5,6},{6,7},{7,8},{8,9},{9,10},{10,1... | collective-permute-start | bytes 196616 | tf_op jit(solution)/shard_map/ppermute | solution.py:20
  424.5 21.3 %collective-permute-start.17 = (bf16[2,1,64,256]{2,3,1,0:T(8,128)(2,1)}, bf16[2,1,64,256]{2,3,1,0:T(8,128)(2,1)}, u32[]{:S(2)}, u32[]{:S(2)}) collective-permute-start(bf16[2,1,64,256]{2,3,1,0:T(8,128)(2,1)} %pad_maximum_fusion.21), channel_id=1, source_target_pairs={{1,0},{2,1},{3,2},{4,3},{5,4},{6,5},{7,6},{8,7},{9,8},{10,9},{11,1... | collective-permute-start | bytes 196616 | tf_op jit(solution)/shard_map/ppermute | solution.py:20
  427.2 26.6 %collective-permute-start.22 = (bf16[1,64,16,64]{1,2,3,0:T(8,128)(2,1)}, bf16[1,64,16,64]{1,2,3,0:T(8,128)(2,1)}, u32[]{:S(2)}, u32[]{:S(2)}) collective-permute-start(bf16[1,64,16,64]{1,2,3,0:T(8,128)(2,1)} %get-tuple-element.158), channel_id=1, source_target_pairs={{1,0},{2,1},{3,2},{4,3},{5,4},{6,5},{7,6},{8,7},{9,8},{10,9},{11,1... | collective-permute-start | bytes 393224 | tf_op jit(solution)/shard_map/ppermute | solution.py:20
  438.9 18.9 %collective-permute-start.20 = (bf16[1,64,16,64]{1,2,3,0:T(8,128)(2,1)S(1)}, bf16[1,64,16,64]{1,2,3,0:T(8,128)(2,1)S(1)}, u32[]{:S(2)}, u32[]{:S(2)}) collective-permute-start(bf16[1,64,16,64]{1,2,3,0:T(8,128)(2,1)S(1)} %copy-done.36), channel_id=1, source_target_pairs={{0,1},{1,2},{2,3},{3,4},{4,5},{5,6},{6,7},{7,8},{8,9},{9,10},{10,1... | collective-permute-start | bytes 393224 | tf_op jit(solution)/shard_map/ppermute | solution.py:20
  444.5 13.3 %collective-permute-start.18 = (bf16[1,64,256]{1,2,0:T(8,128)(2,1)S(1)}, bf16[1,64,256]{1,2,0:T(8,128)(2,1)S(1)}, u32[]{:S(2)}, u32[]{:S(2)}) collective-permute-start(bf16[1,64,256]{1,2,0:T(8,128)(2,1)S(1)} %get-tuple-element.203), channel_id=1, source_target_pairs={{64,0},{96,32},{65,1},{97,33},{66,2},{98,34},{67,3},{99,35},{68,4}... | collective-permute-start | bytes 98312 | tf_op jit(solution)/shard_map/ppermute | solution.py:20
  446.7 11.1 %collective-permute-start.19 = (bf16[1,64,256]{1,2,0:T(8,128)(2,1)S(1)}, bf16[1,64,256]{1,2,0:T(8,128)(2,1)S(1)}, u32[]{:S(2)}, u32[]{:S(2)}) collective-permute-start(bf16[1,64,256]{1,2,0:T(8,128)(2,1)S(1)} %get-tuple-element.205), channel_id=1, source_target_pairs={{0,64},{32,96},{1,65},{33,97},{2,66},{34,98},{3,67},{35,99},{4,68}... | collective-permute-start | bytes 98312 | tf_op jit(solution)/shard_map/ppermute | solution.py:20
  455.0 8.8 collective-permute-start.23
  458.1 10.5 %collective-permute-start.21 = (bf16[2,1,64,16,64]{2,4,3,1,0:T(8,128)(2,1)S(1)}, bf16[2,1,64,16,64]{2,4,3,1,0:T(8,128)(2,1)S(1)}, u32[]{:S(2)}, u32[]{:S(2)}) collective-permute-start(bf16[2,1,64,16,64]{2,4,3,1,0:T(8,128)(2,1)S(1)} %copy.235), channel_id=1, source_target_pairs={{32,0},{64,32},{96,64},{33,1},{65,33},{97,65},{34,2},{66,34},{98,6... | collective-permute-start | bytes 786440 | tf_op jit(solution)/shard_map/ppermute | solution.py:20
  735.1 13.0 %collective-permute-start.24 = (bf16[2,1,64,256]{2,3,1,0:T(8,128)(2,1)S(1)}, bf16[2,1,64,256]{2,3,1,0:T(8,128)(2,1)S(1)}, u32[]{:S(2)}, u32[]{:S(2)}) collective-permute-start(bf16[2,1,64,256]{2,3,1,0:T(8,128)(2,1)S(1)} %pad_maximum_fusion.22), channel_id=1, source_target_pairs={{0,1},{1,2},{2,3},{3,4},{4,5},{5,6},{6,7},{7,8},{8,9},{9,10},{10,1... | collective-permute-start | bytes 196616 | tf_op jit(solution)/shard_map/ppermute | solution.py:20
  739.0 11.0 %collective-permute-start.25 = (bf16[2,1,64,256]{2,3,1,0:T(8,128)(2,1)S(1)}, bf16[2,1,64,256]{2,3,1,0:T(8,128)(2,1)S(1)}, u32[]{:S(2)}, u32[]{:S(2)}) collective-permute-start(bf16[2,1,64,256]{2,3,1,0:T(8,128)(2,1)S(1)} %pad_maximum_fusion.23), channel_id=1, source_target_pairs={{1,0},{2,1},{3,2},{4,3},{5,4},{6,5},{7,6},{8,7},{9,8},{10,9},{11,1... | collective-permute-start | bytes 196616 | tf_op jit(solution)/shard_map/ppermute | solution.py:20
  740.7 15.2 %collective-permute-start.28 = (bf16[1,64,16,64]{1,2,3,0:T(8,128)(2,1)S(1)}, bf16[1,64,16,64]{1,2,3,0:T(8,128)(2,1)S(1)}, u32[]{:S(2)}, u32[]{:S(2)}) collective-permute-start(bf16[1,64,16,64]{1,2,3,0:T(8,128)(2,1)S(1)} %copy-done.37), channel_id=1, source_target_pairs={{0,1},{1,2},{2,3},{3,4},{4,5},{5,6},{6,7},{7,8},{8,9},{9,10},{10,1... | collective-permute-start | bytes 393224 | tf_op jit(solution)/shard_map/ppermute | solution.py:20
  746.8 14.5 %collective-permute-start.30 = (bf16[1,64,16,64]{1,2,3,0:T(8,128)(2,1)S(1)}, bf16[1,64,16,64]{1,2,3,0:T(8,128)(2,1)S(1)}, u32[]{:S(2)}, u32[]{:S(2)}) collective-permute-start(bf16[1,64,16,64]{1,2,3,0:T(8,128)(2,1)S(1)} %get-tuple-element.154), channel_id=1, source_target_pairs={{1,0},{2,1},{3,2},{4,3},{5,4},{6,5},{7,6},{8,7},{9,8},{10,9},{11,1... | collective-permute-start | bytes 393224 | tf_op jit(solution)/shard_map/ppermute | solution.py:20
  748.8 131.8 %collective-permute-start.26 = (bf16[1,64,256]{1,2,0:T(8,128)(2,1)}, bf16[1,64,256]{1,2,0:T(8,128)(2,1)}, u32[]{:S(2)}, u32[]{:S(2)}) collective-permute-start(bf16[1,64,256]{1,2,0:T(8,128)(2,1)} %get-tuple-element.199), channel_id=1, source_target_pairs={{64,0},{96,32},{65,1},{97,33},{66,2},{98,34},{67,3},{99,35},{68,4}... | collective-permute-start | bytes 98312 | tf_op jit(solution)/shard_map/ppermute | solution.py:20
  750.7 129.9 %collective-permute-start.27 = (bf16[1,64,256]{1,2,0:T(8,128)(2,1)}, bf16[1,64,256]{1,2,0:T(8,128)(2,1)}, u32[]{:S(2)}, u32[]{:S(2)}) collective-permute-start(bf16[1,64,256]{1,2,0:T(8,128)(2,1)} %get-tuple-element.201), channel_id=1, source_target_pairs={{0,64},{32,96},{1,65},{33,97},{2,66},{34,98},{3,67},{35,99},{4,68}... | collective-permute-start | bytes 98312 | tf_op jit(solution)/shard_map/ppermute | solution.py:20
  756.8 122.7 %collective-permute-start.29 = (bf16[2,1,64,16,64]{2,3,4,1,0:T(8,128)(2,1)}, bf16[2,1,64,16,64]{2,3,4,1,0:T(8,128)(2,1)S(1)}, u32[]{:S(2)}, u32[]{:S(2)}) collective-permute-start(bf16[2,1,64,16,64]{2,3,4,1,0:T(8,128)(2,1)} %pad_maximum_fusion.10), channel_id=1, source_target_pairs={{32,0},{64,32},{96,64},{33,1},{65,33},{97,65},{34,2},{66,34},{98,6... | collective-permute-start | bytes 786440 | tf_op jit(solution)/shard_map/ppermute | solution.py:20
  762.2 117.3 %collective-permute-start.31 = (bf16[2,1,64,16,64]{2,3,4,1,0:T(8,128)(2,1)}, bf16[2,1,64,16,64]{2,3,4,1,0:T(8,128)(2,1)}, u32[]{:S(2)}, u32[]{:S(2)}) collective-permute-start(bf16[2,1,64,16,64]{2,3,4,1,0:T(8,128)(2,1)} %pad_maximum_fusion.11), channel_id=1, source_target_pairs={{0,32},{32,64},{64,96},{1,33},{33,65},{65,97},{2,34},{34,66},{66,9... | collective-permute-start | bytes 786440 | tf_op jit(solution)/shard_map/ppermute | solution.py:20
  (43 other events, 345.5 us)
Sparse Core Ops, SparseCore 0:
  734.2 143.1 all-reduce.21
where the time goes:
time: 914 us; the launch traced here: 900 us
  local copies, waits for them, and re-layouts  399 us (44%)
  waiting for transfers between devices  142 us (16%)
  other arithmetic  136 us (15%)
  starting transfers between devices  91.7 us (10%)
  blocking collectives  91.7 us (10%)
  between operations  20.4 us (2%)
  matrix products  19.9 us (2%)
    another operation x41, local copies, waits for them, and re-layouts, patches(): return jnp.stack(windows, 0).reshape(9 * channels, edge_bins * edge_bins)  149 us
    psum x1, waiting for transfers between devices, per_device(): lax.psum((jnp.stack(weight_terms), jnp.stack(bias_terms)), ('band', 'pos'))  113 us
    add_any x10, local copies, waits for them, and re-layouts, patches(): lax.dynamic_slice(framed, (anchor, start_row, start_col), (channels, edge...  110 us
    psum x1, blocking collectives, per_device(): lax.psum((jnp.stack(weight_terms), jnp.stack(bias_terms)), ('band', 'pos'))  91.7 us
    ppermute x32, starting transfers between devices, from_behind(): lax.ppermute(value, axis, [(source, source + steps) for source in range(f...  91.6 us
    unnamed x112, local copies, waits for them, and re-layouts  39.2 us
    ppermute x32, waiting for transfers between devices, from_behind(): lax.ppermute(value, axis, [(source, source + steps) for source in range(f...  28.8 us
    reshape x2, local copies, waits for them, and re-layouts, patches(): return jnp.stack(windows, 0).reshape(9 * channels, edge_bins * edge_bins)  26.8 us
  transfers between devices with their start and end apart: 33, of which 8 were waited for; matrix products, arithmetic and copies ran while one was open for 7% of the time, Pallas kernels for 0%

commit v1 on v0

v1 whole, which is shorter than its diff:
```python
import functools
import math

import jax
import jax.numpy as jnp
from jax import lax
from jax.experimental import pallas as pl
from jax.experimental.pallas import tpu as pltpu
from jax.sharding import PartitionSpec as P

BLOCK = 64
DMAX = 16
LAYERS = 2
CH = 64
LANES = 128
HALF = 32
WIDE = BLOCK + 2 * DMAX
F32 = jnp.float32
BF16 = jnp.bfloat16
MESH = pl.DeviceIdType.MESH

STEPS = ((1, -1), (0, -1), (0, 1), (-1, 1), (1, 0), (1, -2), (-1, 2), (-1, 0))
ABOVE, RIGHT, LEFT, BELOW, CORNER_ABOVE, FAR_ABOVE, FAR_BELOW, CORNER_BELOW = range(8)
EDGE_LOW = slice(0, DMAX)
CENTRE = slice(DMAX, DMAX + BLOCK)
EDGE_HIGH = slice(DMAX + BLOCK, WIDE)
SQRT_2_PI = math.sqrt(2.0 / math.pi)
CUBIC = 0.044715


def is_low(shape):
    return lax.broadcasted_iota(jnp.int32, shape, len(shape) - 1) < CH


def swap(value):
    return pltpu.roll(value, CH, value.ndim - 1)


def pick(low_value, high_value):
    return jnp.where(is_low(low_value.shape), low_value, high_value)


def merge(first, second):
    return jnp.concatenate([pick(first, swap(second)), pick(swap(first), second)], axis=0)


def both_gelu(value):
    square = value * value
    inner = SQRT_2_PI * (value + CUBIC * (square * value))
    bend = jnp.tanh(inner)
    cdf = 0.5 * (1.0 + bend)
    slope = cdf + 0.5 * value * (1.0 - bend * bend) * (SQRT_2_PI * (1.0 + 3.0 * CUBIC * square))
    return value * cdf, slope


def net_kernel(
    rows_all,
    offsets_all,
    width_ref,
    dilation_ref,
    input_ref,
    cot_ref,
    weight_ref,
    bias_ref,
    out_ref,
    grad_ref,
    term_ref,
    frame,
    cols,
    slopes,
    slope_low,
    padded,
    grad,
    pair_grad,
    w_fwd,
    w_bwd,
    turn,
    send_a,
    send_b,
    send_l,
    send_r,
    recv_a,
    recv_b,
    recv_l,
    recv_r,
    recv_c,
    send_sem,
    recv_sem,
):
    row = lax.axis_index("pos")
    off = lax.axis_index("band")

    def exists(di, do):
        return (row + di >= 0) & (row + di < rows_all) & (off + do >= 0) & (off + do < offsets_all)

    kept = jnp.where(
        (off <= width_ref[0]) & (row + off < rows_all), jnp.float32(1.0), jnp.float32(0.0)
    )

    views = {
        ABOVE: (send_a, recv_a, CENTRE, CENTRE),
        CORNER_ABOVE: (send_a, recv_c, slice(64, 80), EDGE_LOW),
        FAR_ABOVE: (send_a, recv_c, slice(16, 32), EDGE_HIGH),
        BELOW: (send_b, recv_b, CENTRE, CENTRE),
        FAR_BELOW: (send_b, recv_c, slice(64, 80), EDGE_LOW),
        CORNER_BELOW: (send_b, recv_c, slice(16, 32), EDGE_HIGH),
        LEFT: (send_l, recv_l, slice(0, 16), slice(0, 16)),
        RIGHT: (send_r, recv_r, slice(0, 16), slice(0, 16)),
    }

    for piece in range(8):
        di, do = STEPS[piece]
        target = views[piece][1]
        for sign, indices in ((1, (0, 1)), (-1, (2, 3))):

            @pl.when(jnp.logical_not(exists(-sign * di, -sign * do)))
            def _():
                for index in indices:
                    there = target.at[(index, piece - 4) if piece >= 4 else (index,)]
                    there[...] = jnp.zeros(there.shape, BF16)

    barrier = pltpu.get_barrier_semaphore()
    count = jnp.int32(0)
    for di, do in STEPS:
        count = count + exists(di, do).astype(jnp.int32)

        @pl.when(exists(di, do))
        def _():
            pl.semaphore_signal(
                barrier,
                inc=1,
                device_id={"pos": row + di, "band": off + do},
                device_id_type=MESH,
            )

    def piece_copy(index, piece):
        di, do = STEPS[piece]
        source, target, fwd_part, bwd_part = views[piece]
        there = (index, piece - 4) if piece >= 4 else (index,)
        forward = index < LAYERS
        part = fwd_part if forward else bwd_part
        sign = 1 if forward else -1
        return pltpu.make_async_remote_copy(
            src_ref=source.at[index, :, part, :],
            dst_ref=target.at[there],
            send_sem=send_sem.at[index, piece],
            recv_sem=recv_sem.at[index, piece],
            device_id={"pos": row + sign * di, "band": off + sign * do},
            device_id_type=MESH,
        )

    def send(index, pieces):
        sign = 1 if index < LAYERS else -1
        for piece in pieces:
            di, do = STEPS[piece]

            @pl.when(exists(sign * di, sign * do))
            def _():
                piece_copy(index, piece).start()

    def wait(index, pieces):
        sign = 1 if index < LAYERS else -1
        for piece in pieces:
            di, do = STEPS[piece]

            @pl.when(exists(-sign * di, -sign * do))
            def _():
                piece_copy(index, piece).wait_recv()

    def finish(index):
        sign = 1 if index < LAYERS else -1
        for piece in range(8):
            di, do = STEPS[piece]

            @pl.when(exists(sign * di, sign * do))
            def _():
                piece_copy(index, piece).wait_send()

    def to_tiles(source, k):
        first = source[:, pl.ds(pl.multiple_of(k * LANES, LANES), LANES)].astype(F32)
        second = source[:, pl.ds(pl.multiple_of((k + 16) * LANES, LANES), LANES)].astype(F32)
        return jnp.concatenate([first, second], axis=0).T

    def from_tiles(target, k, first, second):
        turned = jnp.concatenate([first, second], axis=0).T.astype(target.dtype)
        target[:, pl.ds(pl.multiple_of(k * LANES, LANES), LANES)] = turned[:CH]
        target[:, pl.ds(pl.multiple_of((k + 16) * LANES, LANES), LANES)] = turned[CH:]

    def rows_to_cols(load, store):
        @pl.loop(0, 8)
        def _(k):
            turn[pl.ds(pl.multiple_of(k * 64, 64), 64), :] = load(k)

        for t in range(HALF):
            store(t, merge(turn[pl.ds(t, 8, stride=64), :], turn[pl.ds(HALF + t, 8, stride=64), :]))

    def cols_to_rows(load, store):
        @pl.loop(0, HALF)
        def _(t):
            turn[pl.ds(pl.multiple_of(t * 16, 16), 16), :] = load(t)

        for k in range(8):
            store(
                k,
                merge(turn[pl.ds(k, HALF, stride=16), :], turn[pl.ds(8 + k, HALF, stride=16), :]),
            )

    def turn_corner(load, store):
        for k in range(8):
            turn[pl.ds(k * 16, 16), :] = load(k)
        for k in range(8):
            store(k, merge(turn[pl.ds(k, 8, stride=16), :], turn[pl.ds(8 + k, 8, stride=16), :]))

    def pack_forward(index):
        @pl.loop(0, 8)
        def _(k):
            send_a[index, k, CENTRE, :] = pick(
                swap(frame[32 + k, CENTRE, :]), frame[40 + k, CENTRE, :]
            ).astype(BF16)
            send_b[index, k, CENTRE, :] = pick(
                frame[16 + k, CENTRE, :], swap(frame[24 + k, CENTRE, :])
            ).astype(BF16)

        @pl.loop(0, HALF)
        def _(t):
            send_l[index, t] = frame[16 + t, slice(64, 80), :].astype(BF16)
            send_r[index, t] = frame[16 + t, slice(16, 32), :].astype(BF16)

    def unpack_forward(index):
        def put_down_left(k, value):
            recv_c[index, FAR_BELOW - 4, k] = value.astype(BF16)

        @pl.when(off == 0)
        def _():
            def put_left(t, value):
                recv_l[index, t] = value.astype(BF16)

            def put_below(k, value):
                recv_b[index, k] = value.astype(BF16)

            rows_to_cols(lambda k: recv_a[index, k].astype(F32), put_left)
            cols_to_rows(lambda t: recv_r[index, t].astype(F32), put_below)
            turn_corner(
                lambda k: recv_c[index, FAR_ABOVE - 4, k].astype(F32), put_down_left
            )

        @pl.when(off == 1)
        def _():
            turn_corner(
                lambda k: send_a[index, k, slice(16, 32), :].astype(F32), put_down_left
            )

        @pl.loop(0, HALF)
        def _(t):
            frame[16 + t, EDGE_LOW, :] = recv_l[index, t].astype(F32)
            frame[16 + t, EDGE_HIGH, :] = recv_r[index, t].astype(F32)

        @pl.loop(0, 8)
        def _(k):
            above, below = (
                jnp.concatenate(
                    [recv_c[index, low - 4, k], strip[index, k], recv_c[index, high - 4, k]], axis=0
                ).astype(F32)
                for low, strip, high in (
                    (CORNER_ABOVE, recv_a, FAR_ABOVE),
                    (FAR_BELOW, recv_b, CORNER_BELOW),
                )
            )
            frame[k] = pick(above, swap(frame[32 + k]))
            frame[8 + k] = swap(pick(frame[40 + k], above))
            frame[48 + k] = swap(pick(below, frame[16 + k]))
            frame[56 + k] = pick(swap(frame[24 + k]), below)

    def prepare_weights(layer):
        weight = weight_ref[layer].astype(F32)
        pieces = [weight[:, j * LANES : (j + 1) * LANES] for j in range(4)]
        pieces.append(
            jnp.concatenate([weight[:, 512:576], jnp.zeros((CH, CH), F32)], axis=1)
        )
        turned = [jnp.concatenate([piece, piece], axis=0).T for piece in pieces]
        for a in range(3):
            for b in range(3):
                for pair, tap in enumerate((3 * a + b, 3 * b + a)):
                    plain = turned[tap // 2][(tap % 2) * CH : (tap % 2) * CH + CH]
                    low = is_low(plain.shape)
                    at = (3 * a + b) * LANES
                    lane = pair * LANES
                    w_fwd[layer, at : at + CH, lane : lane + LANES] = jnp.where(
                        low, plain, 0.0
                    ).astype(BF16)
                    w_fwd[layer, at + CH : at + LANES, lane : lane + LANES] = jnp.where(
                        low, 0.0, plain
                    ).astype(BF16)
                    own = pieces[tap // 2]
                    other = swap(own)
                    if tap % 2:
                        own, other = other, own
                    at = a * 2 * LANES + pair * LANES
                    lane = b * LANES
                    w_bwd[layer, at : at + CH, lane : lane + LANES] = jnp.where(
                        low, own, 0.0
                    ).astype(BF16)
                    w_bwd[layer, at + CH : at + LANES, lane : lane + LANES] = jnp.where(
                        low, 0.0, other
                    ).astype(BF16)

    def shift_columns(layer):
        spread = dilation_ref[layer]

        @pl.loop(0, 64)
        def _(t):
            for b in range(3):
                cols[layer, t, :, b * LANES : (b + 1) * LANES] = frame[
                    t, pl.ds(DMAX + (b - 1) * spread, BLOCK), :
                ].astype(BF16)

    def taps(layer, t, tiles):
        spread = dilation_ref[layer]
        return [
            cols[layer, pl.ds(DMAX + t + (a - 1) * spread, tiles)].reshape(tiles * BLOCK, 3 * LANES)
            for a in range(3)
        ]

    FWD = 4

    def forward(layer):
        bias = bias_ref[layer : layer + 1, :]
        bias = jnp.concatenate([bias, bias, bias, bias], axis=1)

        @pl.loop(0, HALF // FWD)
        def _(step):
            t = step * FWD
            mixed = (
                jnp.dot(
                    jnp.concatenate(taps(layer, t, FWD), axis=1),
                    w_fwd[layer],
                    preferred_element_type=F32,
                )
                + bias
            )
            value, slope = both_gelu(mixed)
            slopes[layer, pl.ds(t, FWD)] = slope.reshape(FWD, BLOCK, 2 * LANES)
            active = 0.5 * (value[:, :LANES] + value[:, LANES:])
            stored = frame[pl.ds(16 + t, FWD), CENTRE, :].reshape(FWD * BLOCK, LANES)
            result = (kept * (stored + active)).astype(BF16).astype(F32)
            frame[pl.ds(16 + t, FWD), CENTRE, :] = result.reshape(FWD, BLOCK, LANES)

    @pl.loop(0, 16)
    def _(k):
        tiles = (to_tiles(input_ref, k) * kept).astype(BF16).astype(F32)
        frame[16 + 2 * k, CENTRE, :] = tiles[:BLOCK]
        frame[17 + 2 * k, CENTRE, :] = tiles[BLOCK:]

    pack_forward(0)
    pl.semaphore_wait(barrier, count)
    send(0, range(8))
    for layer in range(LAYERS):
        prepare_weights(layer)

    @pl.loop(0, 16)
    def _(k):
        tiles = to_tiles(cot_ref, k)
        grad[2 * k] = tiles[:BLOCK]
        grad[2 * k + 1] = tiles[BLOCK:]

    for layer in range(LAYERS):
        wait(layer, range(8))
        unpack_forward(layer)
        shift_columns(layer)
        forward(layer)
        if layer < LAYERS - 1:
            pack_forward(layer + 1)
            send(layer + 1, range(8))

    @pl.loop(0, 16)
    def _(k):
        from_tiles(out_ref, k, frame[16 + 2 * k, CENTRE, :], frame[17 + 2 * k, CENTRE, :])

    @pl.loop(0, 16)
    def _(t):
        slope_low[t] = jnp.zeros((BLOCK, 2 * LANES), BF16)
        slope_low[48 + t] = jnp.zeros((BLOCK, 2 * LANES), BF16)

    @pl.loop(0, 8)
    def _(t):
        for b in range(3):
            padded[b, t, 0:32, :] = jnp.zeros((32, LANES), F32)
            padded[b, t, 96:128, :] = jnp.zeros((32, LANES), F32)

    def slope_step(layer):
        def step(t, total):
            masked = kept * grad[t]
            grad[t] = masked
            half = 0.5 * masked
            slope = slopes[layer, t] * jnp.concatenate([half, half], axis=1)
            slope_low[16 + t] = slope.astype(BF16)
            return total + jnp.sum(slope.reshape(8, 8, 2 * LANES), axis=0)

        return lax.fori_loop(0, HALF, step, jnp.zeros((8, 2 * LANES), F32))

    BWD = 8

    def tile_grad(layer):
        spread = dilation_ref[layer]

        def part(step, which):
            first = step * BWD
            held = [
                slope_low[pl.ds(first - (a - 1) * spread, BWD)].reshape(BWD * BLOCK, 2 * LANES)
                for a in which
            ]
            left = held[0] if len(held) == 1 else jnp.concatenate(held, axis=1)
            rows = w_bwd[layer, which[0] * 2 * LANES : (which[-1] + 1) * 2 * LANES, :]
            result = jnp.dot(left, rows, preferred_element_type=F32)
            for b in range(3):
                padded[b, :, 32:96, :] = result[:, b * LANES : (b + 1) * LANES].reshape(
                    BWD, BLOCK, LANES
                )
            for at in range(BWD):
                total = None
                for b in range(3):
                    term = padded[b, at, pl.ds(DMAX - (b - 1) * spread, WIDE), :]
                    total = term if total is None else total + term
                frame[first + at] = total

        @pl.loop(0, 2)
        def _(step):
            part(step, (0,))

        @pl.loop(2, 6)
        def _(step):
            part(step, (0, 1, 2))

        @pl.loop(6, 8)
        def _(step):
            part(step, (2,))

    def pack_backward(index):
        @pl.loop(0, 8)
        def _(k):
            above = pick(frame[k], swap(frame[8 + k]))
            below = pick(swap(frame[48 + k]), frame[56 + k])
            low = is_low(above.shape)
            frame[16 + k] = frame[16 + k] + jnp.where(low, 0.0, swap(frame[48 + k]))
            frame[24 + k] = frame[24 + k] + jnp.where(low, 0.0, swap(frame[56 + k]))
            frame[32 + k] = frame[32 + k] + jnp.where(low, swap(frame[k]), 0.0)
            frame[40 + k] = frame[40 + k] + jnp.where(low, swap(frame[8 + k]), 0.0)
            frame[k] = above
            frame[48 + k] = below

        @pl.when(off == 0)
        def _():
            def add_above(k, value):
                frame[k, CENTRE, :] = frame[k, CENTRE, :] + value

            def add_right(t, value):
                frame[16 + t, EDGE_HIGH, :] = frame[16 + t, EDGE_HIGH, :] + value

            def add_far(k, value):
                frame[k, EDGE_HIGH, :] = frame[k, EDGE_HIGH, :] + value

            cols_to_rows(lambda t: frame[16 + t, EDGE_LOW, :], add_above)
            rows_to_cols(lambda k: frame[48 + k, CENTRE, :], add_right)
            turn_corner(lambda k: frame[48 + k, EDGE_LOW, :], add_far)

        @pl.when(off == 1)
        def _():
            def add_own(k, value):
                low = is_low(value.shape)
                at = slice(16, 32)
                frame[32 + k, at, :] = frame[32 + k, at, :] + jnp.where(low, 0.0, swap(value))
                frame[40 + k, at, :] = frame[40 + k, at, :] + jnp.where(low, 0.0, value)

            turn_corner(lambda k: frame[48 + k, EDGE_LOW, :], add_own)

        @pl.loop(0, 8)
        def _(k):
            send_a[index, k] = frame[k].astype(BF16)
            send_b[index, k] = frame[48 + k].astype(BF16)

        @pl.loop(0, HALF)
        def _(t):
            send_l[index, t] = frame[16 + t, EDGE_LOW, :].astype(BF16)
            send_r[index, t] = frame[16 + t, EDGE_HIGH, :].astype(BF16)

    def unpack_backward(index):
        @pl.loop(0, HALF)
        def _(t):
            total = grad[t] + frame[16 + t, CENTRE, :]
            right = recv_r[index, t].astype(F32)
            left = recv_l[index, t].astype(F32)
            edge = jnp.concatenate([right, jnp.zeros((32, LANES), F32), left], axis=0)
            grad[t] = total + edge

        @pl.loop(0, 8)
        def _(k):
            def strip(ref, low, high):
                corners = [
                    recv_c[index, high - 4, k].astype(F32),
                    jnp.zeros((32, LANES), F32),
                    recv_c[index, low - 4, k].astype(F32),
                ]
                return ref[index, k].astype(F32) + jnp.concatenate(corners, axis=0)

            top = strip(recv_b, FAR_BELOW, CORNER_BELOW)
            bottom = strip(recv_a, CORNER_ABOVE, FAR_ABOVE)
            low = is_low(top.shape)
            grad[k] = grad[k] + jnp.where(low, top, 0.0)
            grad[8 + k] = grad[8 + k] + jnp.where(low, swap(top), 0.0)
            grad[16 + k] = grad[16 + k] + jnp.where(low, 0.0, swap(bottom))
            grad[24 + k] = grad[24 + k] + jnp.where(low, 0.0, bottom)

    PG = 8

    def weight_terms(layer, bias_rows):
        pair_grad[...] = jnp.zeros_like(pair_grad)

        @pl.loop(0, HALF // PG)
        def _(step):
            t = step * PG
            left = slope_low[pl.ds(16 + t, PG)].reshape(PG * BLOCK, 2 * LANES)
            for a, part in enumerate(taps(layer, t, PG)):
                lane = a * 3 * LANES
                pair_grad[:, lane : lane + 3 * LANES] += lax.dot_general(
                    left, part, (((0,), (0,)), ((), ())), preferred_element_type=F32
                )

        def tap_part(tap, half):
            turned = 3 * (tap % 3) + tap // 3
            first = pair_grad[half * CH : half * CH + CH, tap * LANES : (tap + 1) * LANES]
            at = LANES + half * CH
            second = pair_grad[at : at + CH, turned * LANES : (turned + 1) * LANES]
            return first + second

        for j in range(5):
            low_part = tap_part(2 * j, 0) + swap(tap_part(2 * j, 1))
            if j < 4:
                high_part = tap_part(2 * j + 1, 1) + swap(tap_part(2 * j + 1, 0))
            else:
                total = jnp.sum(bias_rows, axis=0, keepdims=True)
                total = total[:, :LANES] + total[:, LANES:]
                total = total + swap(total)
                high_part = jnp.broadcast_to(total, (LANES, LANES)).T[:CH]
            term_ref[layer * CH : (layer + 1) * CH, j * LANES : (j + 1) * LANES] = pick(
                low_part, high_part
            )

    for layer in reversed(range(LAYERS)):
        index = 2 * LAYERS - 1 - layer
        bias_rows = slope_step(layer)
        tile_grad(layer)
        pack_backward(index)
        send(index, range(8))
        weight_terms(layer, bias_rows)
        wait(index, range(8))
        unpack_backward(index)

    @pl.loop(0, 16)
    def _(k):
        from_tiles(grad_ref, k, kept * grad[2 * k], kept * grad[2 * k + 1])

    for index in range(2 * LAYERS):
        finish(index)


def sum_kernel(
    group, outer, offsets_all, scale, term_ref, weight_ref, bias_ref, slots, shards, whole, send_sem, recv_sem
):
    pos = lax.axis_index("pos")
    band = lax.axis_index("band")
    inner = lax.rem(pos, group)
    high = lax.div(pos, group)
    rows = term_ref.shape[0] // group
    many = outer * offsets_all
    mine = high * offsets_all + band

    def in_plane(step):
        other = lax.rem(inner + step, group)
        return other, {"pos": high * group + other, "band": band}

    def across(step):
        other = lax.rem(mine + step, many)
        return other, {
            "pos": lax.div(other, offsets_all) * group + inner,
            "band": lax.rem(other, offsets_all),
        }

    barrier = pltpu.get_barrier_semaphore()
    for step in range(1, group):
        pl.semaphore_signal(barrier, inc=1, device_id=in_plane(step)[1], device_id_type=MESH)
    for step in range(1, many):
        pl.semaphore_signal(barrier, inc=1, device_id=across(step)[1], device_id_type=MESH)
    pl.semaphore_wait(barrier, group + many - 2)

    def span(at):
        return pl.ds(pl.multiple_of(at * rows, rows), rows)

    copies = []
    for step in range(1, group):
        other, device = in_plane(step)
        copies.append(
            pltpu.make_async_remote_copy(
                src_ref=term_ref.at[span(other)],
                dst_ref=slots.at[step],
                send_sem=send_sem.at[0, step],
                recv_sem=recv_sem.at[0, step],
                device_id=device,
                device_id_type=MESH,
            )
        )
        copies[-1].start()
    total = term_ref[span(inner)]
    for step in range(1, group):
        copies[step - 1].wait_recv()
        total = total + slots[step]
    shards[mine] = total
    seconds = []
    for step in range(1, many):
        other, device = across(step)
        seconds.append(
            pltpu.make_async_remote_copy(
                src_ref=shards.at[mine],
                dst_ref=shards.at[mine],
                send_sem=send_sem.at[1, step],
                recv_sem=recv_sem.at[1, step],
                device_id=device,
                device_id_type=MESH,
            )
        )
        seconds[-1].start()
    for copy in seconds:
        copy.wait_recv()
    total = shards[0]
    for at in range(1, many):
        total = total + shards[at]
    whole[inner] = total * scale
    thirds = []
    for step in range(1, group):
        other, device = in_plane(step)
        thirds.append(
            pltpu.make_async_remote_copy(
                src_ref=whole.at[inner],
                dst_ref=whole.at[inner],
                send_sem=send_sem.at[2, step],
                recv_sem=recv_sem.at[2, step],
                device_id=device,
                device_id_type=MESH,
            )
        )
        thirds[-1].start()
    for copy in thirds:
        copy.wait_recv()
    result = whole[...].reshape(group * rows, 5 * LANES)
    for layer in range(LAYERS):
        weight_ref[layer] = result[layer * CH : (layer + 1) * CH, :576]
    column = result[:, 4 * LANES :].T[CH : CH + 1]
    bias_ref[0:1, :] = column[:, :CH]
    bias_ref[1:2, :] = swap(column)[:, :CH]
    for copy in copies + seconds + thirds:
        copy.wait_send()


def per_device(input_map, cotangent, band_width, dilation, conv_weight, conv_bias):
    rows_all = lax.axis_size("pos")
    offsets_all = lax.axis_size("band")
    bins = BLOCK * BLOCK
    vmem = pl.BlockSpec(memory_space=pltpu.VMEM)
    smem = pl.BlockSpec(memory_space=pltpu.SMEM)
    output, input_grad, terms = pl.pallas_call(
        functools.partial(net_kernel, rows_all, offsets_all),
        out_shape=(
            jax.ShapeDtypeStruct((CH, bins), BF16),
            jax.ShapeDtypeStruct((CH, bins), F32),
            jax.ShapeDtypeStruct((LAYERS * CH, 5 * LANES), F32),
        ),
        in_specs=[smem, smem, vmem, vmem, vmem, vmem],
        out_specs=(vmem, vmem, vmem),
        scratch_shapes=[
            pltpu.VMEM((64, WIDE, LANES), F32),
            pltpu.VMEM((LAYERS, 64, BLOCK, 3 * LANES), BF16),
            pltpu.VMEM((LAYERS, HALF, BLOCK, 2 * LANES), F32),
            pltpu.VMEM((64, BLOCK, 2 * LANES), BF16),
            pltpu.VMEM((3, 8, 128, LANES), F32),
            pltpu.VMEM((HALF, BLOCK, LANES), F32),
            pltpu.VMEM((2 * LANES, 9 * LANES), F32),
            pltpu.VMEM((LAYERS, 9 * LANES, 2 * LANES), BF16),
            pltpu.VMEM((LAYERS, 6 * LANES, 3 * LANES), BF16),
            pltpu.VMEM((512, LANES), F32),
            pltpu.VMEM((4, 8, WIDE, LANES), BF16),
            pltpu.VMEM((4, 8, WIDE, LANES), BF16),
            pltpu.VMEM((4, HALF, DMAX, LANES), BF16),
            pltpu.VMEM((4, HALF, DMAX, LANES), BF16),
            pltpu.VMEM((4, 8, BLOCK, LANES), BF16),
            pltpu.VMEM((4, 8, BLOCK, LANES), BF16),
            pltpu.VMEM((4, HALF, DMAX, LANES), BF16),
            pltpu.VMEM((4, HALF, DMAX, LANES), BF16),
            pltpu.VMEM((4, 4, 8, DMAX, LANES), BF16),
            pltpu.SemaphoreType.DMA((4, 8)),
            pltpu.SemaphoreType.DMA((4, 8)),
        ],
        compiler_params=pltpu.CompilerParams(collective_id=0, has_side_effects=True),
        name="net",
    )(
        band_width,
        dilation,
        input_map.reshape(CH, bins),
        cotangent.reshape(CH, bins),
        conv_weight,
        conv_bias,
    )
    group = 16 if rows_all % 16 == 0 else rows_all
    outer = rows_all // group
    rows = LAYERS * CH // group
    scale = 1.0 / (BLOCK * math.sqrt(input_map.shape[0] * rows_all * offsets_all))
    weight_grad, bias_grad = pl.pallas_call(
        functools.partial(sum_kernel, group, outer, offsets_all, scale),
        out_shape=(
            jax.ShapeDtypeStruct((LAYERS, CH, 576), F32),
            jax.ShapeDtypeStruct((LAYERS, CH), F32),
        ),
        in_specs=[vmem],
        out_specs=(vmem, vmem),
        scratch_shapes=[
            pltpu.VMEM((group, rows, 5 * LANES), F32),
            pltpu.VMEM((outer * offsets_all, rows, 5 * LANES), F32),
            pltpu.VMEM((group, rows, 5 * LANES), F32),
            pltpu.SemaphoreType.DMA((3, 16)),
            pltpu.SemaphoreType.DMA((3, 16)),
        ],
        compiler_params=pltpu.CompilerParams(collective_id=1, has_side_effects=True),
        name="sum",
    )(terms)
    return (
        output.reshape(input_map.shape),
        input_grad.reshape(input_map.shape),
        weight_grad,
        bias_grad,
    )


def solution(mesh):
    split = P(None, "pos", "band", None, None)
    return jax.shard_map(
        per_device,
        mesh=mesh,
        in_specs=(split, split, P("pos"), P(), P(), P()),
        out_specs=(split, split, P(), P()),
        check_vma=False,
    )
```

time: 914 us -> 102 us (0.11); the launches traced: 900 us -> 102 us
  local copies, waits for them, and re-layouts: 399 us -> 4.32 us
  waiting for transfers between devices: 142 us -> 0 us
  other arithmetic: 136 us -> 0 us
  Pallas kernels: 0 us -> 95.9 us
  blocking collectives: 91.7 us -> 0 us
  starting transfers between devices: 91.7 us -> 0 us
  matrix products: 19.9 us -> 0 us
  between operations: 20.4 us -> 1.31 us
    another operation x54 -> x0, local copies, waits for them, and re-layouts: 156 us -> none  [the longest x41 149 us: patches(): return jnp.stack(windows, 0).reshape(9 * channels, edge_bins * edge_bins)]
    psum x1 -> x0, waiting for transfers between devices: 113 us -> none  [per_device(): lax.psum((jnp.stack(weight_terms), jnp.stack(bias_terms)), ('band', 'pos'))]
    add_any x10 -> x0, local copies, waits for them, and re-layouts: 110 us -> none  [patches(): lax.dynamic_slice(framed, (anchor, start_row, start_col), (channels, edge...]
    pallas_call x0 -> x2, Pallas kernels: none -> 95.9 us  [the longest x1 61.7 us: per_device(): pl.pallas_call(functools.partial(net_kernel, rows_all, offsets_all), out_...]
    psum x1 -> x0, blocking collectives: 91.7 us -> none  [per_device(): lax.psum((jnp.stack(weight_terms), jnp.stack(bias_terms)), ('band', 'pos'))]
    ppermute x32 -> x0, starting transfers between devices: 91.6 us -> none  [from_behind(): lax.ppermute(value, axis, [(source, source + steps) for source in range(f...]
    unnamed x112 -> x10, local copies, waits for them, and re-layouts: 39.2 us -> 4.32 us
    reshape x6 -> x0, local copies, waits for them, and re-layouts: 33.3 us -> none  [the longest x2 26.8 us: patches(): return jnp.stack(windows, 0).reshape(9 * channels, edge_bins * edge_bins)]
  transfers between devices with their start and end apart: 33 -> 0, of which waited for: 8 -> 0; matrix products, arithmetic and copies ran while one was open for 7% -> 0% of each run, Pallas kernels for 0% -> 0%
where the time goes in v1:
time: 102 us
  Pallas kernels  95.9 us (94%)
  local copies, waits for them, and re-layouts  4.32 us (4%)
  between operations  1.31 us (1%)
    pallas_call x1, Pallas kernels, per_device(): pl.pallas_call(functools.partial(net_kernel, rows_all, offsets_all), out_...  61.7 us
    pallas_call x1, Pallas kernels, per_device(): pl.pallas_call(functools.partial(sum_kernel, group, outer, offsets_all, s...  34.2 us
    unnamed x10, local copies, waits for them, and re-layouts  4.32 us

profile of v1, /device:TPU:1, one launch (start us, length us, event | category | flops | bytes accessed | tf_op | source)
XLA Modules:
  0.0 101.5 jit_solution(4946862254356115115)
XLA Ops:
  1.3 61.7 %net.1 = (bf16[64,4096]{1,0:T(8,128)(2,1)}, f32[64,4096]{1,0:T(8,128)}, f32[128,640]{1,0:T(8,128)}) custom-call(s32[1]{0:T(128)S(6)} %copy.14.width_ref, s32[2]{0:T(128)} %dilation_ref.1, bf16[64,4096]{1,0:T(8,128)(2,1)} %bitcast.5, bf16[64,4096]{1,0:T(8,128)(2,1)} %bitcast.6, bf16[2,64,576]{2,1,0:T(8,128)(2,1)} %weight_ref.1, f32[2,64]{1,0:T(2,128)} %bias_ref.1), custom_call_target="tpu_custom_call" | custom-call | tf_op jit(solution)/shard_map/net/pallas_call | solution.py:669
  63.0 0.0 copy-start
  63.0 34.2 %sum.1 = (f32[2,64,576]{2,1,0:T(8,128)}, f32[2,64]{1,0:T(2,128)}) custom-call(f32[128,640]{1,0:T(8,128)} %get-tuple-element.11.term_ref), custom_call_target="tpu_custom_call" | custom-call | tf_op jit(solution)/shard_map/sum/pallas_call | solution.py:715
  97.2 1.9 %copy.15 = bf16[1,1,1,64,4096]{4,3,2,1,0:T(8,128)(2,1)} copy(bf16[1,1,1,64,4096]{4,3,2,1,0:T(8,128)(2,1)} %bitcast.7) | data formatting | bytes 1048576
  99.1 0.0 copy-done
  99.1 0.0 copy-start.1
  99.1 1.0 copy.16
  100.1 0.2 copy-done.1
  100.2 0.0 copy-start.2
  100.2 0.7 copy.17
  101.0 0.0 copy-done.2
  101.0 0.6 copy.18
Async XLA Ops:
  63.0 36.1 %copy-start = (f32[64,4096]{1,0:T(8,128)S(1)}, f32[64,4096]{1,0:T(8,128)}, u32[]{:S(2)}) copy-start(f32[64,4096]{1,0:T(8,128)} %get-tuple-element.10) | copy-start | bytes 3145732
  99.1 1.2 %copy-start.1 = (f32[2,64,576]{2,1,0:T(8,128)S(1)}, f32[2,64,576]{2,1,0:T(8,128)}, u32[]{:S(2)}) copy-start(f32[2,64,576]{2,1,0:T(8,128)} %get-tuple-element.20) | copy-start | bytes 884740
  100.2 0.7 copy-start.2
